TPU v7x, 256 devices: a whole 4x4x8 slice. The times are simulated.
256 devices in a mesh: ab: 16 (over z_lo, y, core), cd: 16 (over z_hi, x).
Axes of the slice: x: 4, y: 4, z: 8 (z_hi: 4, z_lo: 2; z = z_hi * 2 + z_lo), core: 2. Of those that a mesh axis runs over, the one named last changes fastest.
Arguments:
- pair_values: bfloat16 [32768, 32768], P('ab', 'cd'), may hold values from -0.046875 to 0.046875
- amplitudes: bfloat16 [64, 800, 800], P('ab', 'cd'), may hold values from -6 to 6
- cd_first: int32 [32768], P('cd'), may hold values from 0 to 799, as said below
- cd_second: int32 [32768], P('cd'), may hold values from 0 to 799, as said below
- live_cols: int32 [16], P('cd'), may hold values from 512 to 2048, as said below
Outputs:
- ladder: bfloat16 [64, 32768], P(None, ('ab', 'cd'))
Inputs may be any that keep to these rules, and one draw needn't show every extreme that they name: `cd_first`: slot n lies in slab s = n // 2048 and its c lies in orbitals s * 50 to (s + 1) * 50 - 1. cd_second[n] >= cd_first[n] for every slot. `live_cols`: slots 0 and 1 of every slab are live.
All inputs are finite; a program needn't handle non-finite values.
Results may differ from a plain program's by a relative error of at most 0.0051.
Values may be sent and summed in bfloat16 or wider, within the bound.
A program may use at most 64 MiB of HBM per device.

v0:
```python
import jax
import jax.numpy as jnp
from jax import lax
from jax.sharding import PartitionSpec as P


def on_device(pair_values, amplitudes, cd_first, cd_second, live_cols):
    slab = lax.axis_index("cd")
    pair_block = amplitudes.shape[0]
    orbit_block = amplitudes.shape[1]
    orbitals = amplitudes.shape[2]
    columns = cd_first.shape[0]
    local_first = cd_first - slab * orbit_block
    own_flat = amplitudes.reshape(pair_block, orbit_block * orbitals)
    direct = jnp.take(own_flat, local_first * orbitals + cd_second, axis=1)
    whole = lax.all_gather(amplitudes, "cd", axis=1, tiled=True)
    whole_flat = whole.reshape(pair_block, orbitals * orbitals)
    crossed = jnp.take(whole_flat, cd_second * orbitals + cd_first, axis=1)
    live_count = live_cols[0]
    slots = jnp.arange(columns, dtype=jnp.int32)
    live = (slots < live_count).astype(jnp.float32)
    half = jnp.where(cd_first == cd_second, jnp.float32(0.5), jnp.float32(1.0))
    weight = half * live
    packed = ((direct.astype(jnp.float32) + crossed.astype(jnp.float32)) * weight[None, :]).astype(
        jnp.bfloat16
    )
    contract = (((1,), (1,)), ((), ()))
    partial_sums = lax.dot_general(
        lax.all_gather(packed, "ab", axis=0, tiled=True),
        pair_values,
        contract,
        preferred_element_type=jnp.float32,
    )
    return lax.psum_scatter(partial_sums, "cd", scatter_dimension=1, tiled=True).astype(
        jnp.bfloat16
    )


def solution(mesh):
    placed = (P("ab", "cd"), P("ab", "cd", None), P("cd"), P("cd"), P("cd"))
    return jax.shard_map(
        on_device, mesh=mesh, in_specs=placed, out_specs=P(None, ("ab", "cd")), check_vma=False
    )
```

profile of v0, /device:TPU:8, one launch (start us, length us, event | category | flops | bytes accessed | tf_op | source)
XLA Modules:
  0.0 270.1 jit_solution(3929936494071455766)
XLA Ops:
  6.5 0.0 copy-start.1
  6.5 0.0 copy-start
  6.5 0.0 all-gather.3.cloned.1.call-start
  6.5 0.7 all-gather.3.cloned.1.call-update
  7.3 0.0 reduce-scatter.2.cloned.1.call-start
  7.3 8.0 %copy.29 = bf16[4,50,800]{0,2,1:T(8,128)(2,1)} copy(bf16[4,50,800]{2,0,1:T(4,128)(2,1)} %param.6) | data formatting | bytes 640000 | tf_op args[1]
  15.9 0.0 copy-done.1
  15.9 0.0 copy-done
  16.0 10.8 %gather_fusion = bf16[2048,4]{1,0:T(8,128)(2,1)S(1)} fusion(bf16[4,40000]{0,1:T(8,128)(2,1)} %bitcast.9, s32[2048]{0:T(1024)S(1)} %get-tuple-element.7), kind=kCustom, calls=%fused_computation | custom fusion | bytes 40960 | tf_op jit(solution)/shard_map/jit(_take)/gather | solution.py:15
  26.8 0.2 copy.30
  27.0 70.5 %all-gather.3.cloned.1.call-done = bf16[4,800,800]{2,0,1:T(4,128)(2,1)} async-done(((bf16[4,50,800]{2,0,1:T(4,128)(2,1)}), bf16[4,800,800]{2,0,1:T(4,128)(2,1)}) %all-gather.3.cloned.1.call-update) | async-done | bytes 5120016 | tf_op jit(solution)/shard_map/all_gather | solution.py:16
  97.6 5.8 %copy.31 = bf16[4,800,800]{2,1,0:T(8,128)(2,1)} copy(bf16[4,800,800]{2,0,1:T(4,128)(2,1)} %all-gather.3.cloned.1.call-done) | data formatting | bytes 10240000 | tf_op jit(solution)/shard_map/all_gather | solution.py:16
  103.4 12.8 %reshape.39 = bf16[2560000]{0:T(1024)(128)(2,1)} reshape(bf16[4,800,800]{2,1,0:T(8,128)(2,1)} %copy.31) | data formatting | bytes 10240000
  116.2 6.6 %reshape.18 = bf16[4,640000]{1,0:T(4,128)(2,1)} reshape(bf16[2560000]{0:T(1024)(128)(2,1)} %reshape.39) | data formatting | bytes 10240000 | tf_op jit(solution)/shard_map/reshape | solution.py:17
  122.8 23.2 %gather_fusion.1 = bf16[2048,4]{0,1:T(4,128)(2,1)S(1)} fusion(bf16[4,640000]{1,0:T(4,128)(2,1)} %reshape.18, s32[2048]{0:T(1024)S(1)} %get-tuple-element.8), kind=kCustom, calls=%fused_computation.1 | custom fusion | bytes 40960 | tf_op jit(solution)/shard_map/jit(_take)/gather | solution.py:18
  146.1 24.5 %all-gather = bf16[16,4,2048]{2,1,0:T(4,128)(2,1)S(1)} all-gather(bf16[1,4,2048]{2,1,0:T(4,128)(2,1)S(1)} %fusion), channel_id=1, replica_groups=mesh['ab'=16,'cd'=16] {'ab'}, dimensions={0}, use_global_device_ids=true | all-gather | bytes 278528 | tf_op jit(solution)/shard_map/all_gather | solution.py:29
  170.6 0.1 reshape.38
  170.7 6.8 %fusion.1 = f32[64,2048]{1,0:T(8,128)} fusion(bf16[64,2048]{1,0:T(8,128)(2,1)S(1)} %reshape.38, bf16[2048,2048]{1,0:T(8,128)(2,1)} %param.5), kind=kOutput, calls=%fused_computation.12 | convolution fusion | flops 536870912 | bytes 9175040 | tf_op jit(solution)/shard_map/dot_general | solution.py:28
  177.5 0.0 reduce-scatter.2.cloned.1.call-update
  177.5 84.4 %reduce-scatter.2.cloned.1.call-done = f32[64,128]{1,0:T(8,128)} async-done(((f32[64,2048]{1,0:T(8,128)}), f32[64,128]{1,0:T(8,128)}) %reduce-scatter.2.cloned.1.call-update) | async-done | bytes 32784 | tf_op jit(solution)/shard_map/reduce_scatter | solution.py:34
  261.9 1.4 convert_element_type.16
  (4 shorter events, 0.1 us)
Async XLA Ops:
  6.5 9.4 %copy-start.1 = (s32[2048]{0:T(1024)S(1)}, s32[2048]{0:T(1024)}, u32[]{:S(2)}) copy-start(s32[2048]{0:T(1024)} %param.8) | copy-start | bytes 24580
  6.5 9.4 %copy-start = (s32[2048]{0:T(1024)S(1)}, s32[2048]{0:T(1024)}, u32[]{:S(2)}) copy-start(s32[2048]{0:T(1024)} %param.7) | copy-start | bytes 24580
  6.5 91.1 %all-gather.3.cloned.1.call-start = ((), (), s32[]{:S(2)}) async-start(), calls=%async_computation.1 | async-start | bytes 6092800 | tf_op jit(solution)/shard_map/all_gather | solution.py:16
  7.3 254.6 %reduce-scatter.2.cloned.1.call-start = ((), (), s32[]{:S(2)}) async-start(), calls=%async_computation.2 | async-start | bytes 557056 | tf_op jit(solution)/shard_map/reduce_scatter | solution.py:34
Sparse Core Ops, SparseCore 0:
  9.8 87.7 all-gather.2
  177.7 84.2 reduce-scatter.1
where the time goes:
time: 271 us; the launch traced here: 270 us
  waiting for transfers between devices  156 us (58%)
  local copies, waits for them, and re-layouts  67.6 us (25%)
  blocking collectives  24.5 us (9%)
  between operations  14.1 us (5%)
  matrix products  6.83 us (3%)
    reduce_scatter x1, waiting for transfers between devices, on_device(): lax.psum_scatter(partial_sums, 'cd', scatter_dimension=1, tiled=True)  84.4 us
    all_gather x1, waiting for transfers between devices, on_device(): whole = lax.all_gather(amplitudes, 'cd', axis=1, tiled=True)  70.5 us
    all_gather x1, blocking collectives, on_device(): lax.all_gather(packed, 'ab', axis=0, tiled=True)  24.5 us
    gather x1, local copies, waits for them, and re-layouts, on_device(): crossed = jnp.take(whole_flat, cd_second * orbitals + cd_first, axis=1)  23.2 us
    unnamed x7, local copies, waits for them, and re-layouts  20.9 us
    gather x2, local copies, waits for them, and re-layouts, on_device(): direct = jnp.take(own_flat, local_first * orbitals + cd_second, axis=1)  11 us
    dot_general x1, matrix products, on_device(): lax.dot_general(lax.all_gather(packed, 'ab', axis=0, tiled=True), pair_va...  6.83 us
    reshape x1, local copies, waits for them, and re-layouts, on_device(): whole_flat = whole.reshape(pair_block, orbitals * orbitals)  6.61 us
  transfers between devices with their start and end apart: 2, of which 2 were waited for; matrix products, arithmetic and copies ran while one was open for 7% of the time, Pallas kernels for 0%

commit v1 on v0

--- a/solution.py
+++ b/solution.py
@@ -26,7 +26,9 @@
     )
     contract = (((1,), (1,)), ((), ()))
     partial_sums = lax.dot_general(
-        lax.all_gather(packed, "ab", axis=0, tiled=True),
+        jnp.concatenate(
+            lax.all_to_all(jnp.stack([packed] * lax.axis_size("ab")), "ab", 0, 0), axis=0
+        ),
         pair_values,
         contract,
         preferred_element_type=jnp.float32,

time: 271 us -> 264 us (0.974)
  blocking collectives: 24.5 us -> 18 us
    all_gather x1 -> x0, blocking collectives: 24.5 us -> none  [on_device(): lax.all_gather(packed, 'ab', axis=0, tiled=True)]
    all_to_all x0 -> x1, blocking collectives: none -> 18 us  [on_device(): lax.all_to_all(jnp.stack([packed] * lax.axis_size('ab')), 'ab', 0, 0)]
    unnamed x7 -> x6, local copies, waits for them, and re-layouts: 20.9 us -> 20.8 us
where the time goes in v1:
time: 264 us; the launch traced here: 263 us
  waiting for transfers between devices  155 us (59%)
  local copies, waits for them, and re-layouts  67.7 us (26%)
  blocking collectives  18 us (7%)
  between operations  14.1 us (5%)
  matrix products  6.83 us (3%)
    reduce_scatter x1, waiting for transfers between devices, on_device(): lax.psum_scatter(partial_sums, 'cd', scatter_dimension=1, tiled=True)  83.9 us
    all_gather x1, waiting for transfers between devices, on_device(): whole = lax.all_gather(amplitudes, 'cd', axis=1, tiled=True)  70.5 us
    gather x1, local copies, waits for them, and re-layouts, on_device(): crossed = jnp.take(whole_flat, cd_second * orbitals + cd_first, axis=1)  23.2 us
    unnamed x6, local copies, waits for them, and re-layouts  20.8 us
    all_to_all x1, blocking collectives, on_device(): lax.all_to_all(jnp.stack([packed] * lax.axis_size('ab')), 'ab', 0, 0)  18 us
    gather x2, local copies, waits for them, and re-layouts, on_device(): direct = jnp.take(own_flat, local_first * orbitals + cd_second, axis=1)  11 us
    dot_general x1, matrix products, on_device(): lax.dot_general(jnp.concatenate(lax.all_to_all(jnp.stack([packed] * lax.a...  6.83 us
    reshape x1, local copies, waits for them, and re-layouts, on_device(): whole_flat = whole.reshape(pair_block, orbitals * orbitals)  6.61 us
  transfers between devices with their start and end apart: 2, of which 2 were waited for; matrix products, arithmetic and copies ran while one was open for 7% of the time, Pallas kernels for 0%

profile of v1, /device:TPU:8, one launch (start us, length us, event | category | flops | bytes accessed | tf_op | source)
XLA Modules:
  0.0 263.2 jit_solution(13937318981297233874)
XLA Ops:
  6.5 0.0 copy-start.1
  6.5 0.0 copy-start
  6.5 0.0 all-gather.2.cloned.1.call-start
  6.5 0.7 all-gather.2.cloned.1.call-update
  7.3 0.0 reduce-scatter.2.cloned.1.call-start
  7.3 8.0 %copy.22 = bf16[4,50,800]{0,2,1:T(8,128)(2,1)} copy(bf16[4,50,800]{2,0,1:T(4,128)(2,1)} %param.6) | data formatting | bytes 640000 | tf_op args[1]
  15.9 0.0 copy-done.1
  15.9 0.0 copy-done
  16.0 10.8 %gather_fusion = bf16[2048,4]{1,0:T(8,128)(2,1)S(1)} fusion(bf16[4,40000]{0,1:T(8,128)(2,1)} %bitcast.7, s32[2048]{0:T(1024)S(1)} %get-tuple-element.7), kind=kCustom, calls=%fused_computation | custom fusion | bytes 40960 | tf_op jit(solution)/shard_map/jit(_take)/gather | solution.py:15
  26.8 0.2 copy.23
  27.0 70.5 %all-gather.2.cloned.1.call-done = bf16[4,800,800]{2,0,1:T(4,128)(2,1)} async-done(((bf16[4,50,800]{2,0,1:T(4,128)(2,1)}), bf16[4,800,800]{2,0,1:T(4,128)(2,1)}) %all-gather.2.cloned.1.call-update) | async-done | bytes 5120016 | tf_op jit(solution)/shard_map/all_gather | solution.py:16
  97.6 5.8 %copy.24 = bf16[4,800,800]{2,1,0:T(8,128)(2,1)} copy(bf16[4,800,800]{2,0,1:T(4,128)(2,1)} %all-gather.2.cloned.1.call-done) | data formatting | bytes 10240000 | tf_op jit(solution)/shard_map/all_gather | solution.py:16
  103.4 12.8 %reshape.71 = bf16[2560000]{0:T(1024)(128)(2,1)} reshape(bf16[4,800,800]{2,1,0:T(8,128)(2,1)} %copy.24) | data formatting | bytes 10240000
  116.2 6.6 %reshape.51 = bf16[4,640000]{1,0:T(4,128)(2,1)} reshape(bf16[2560000]{0:T(1024)(128)(2,1)} %reshape.71) | data formatting | bytes 10240000 | tf_op jit(solution)/shard_map/reshape | solution.py:17
  122.8 23.2 %gather_fusion.1 = bf16[2048,4]{0,1:T(4,128)(2,1)S(1)} fusion(bf16[4,640000]{1,0:T(4,128)(2,1)} %reshape.51, s32[2048]{0:T(1024)S(1)} %get-tuple-element.8), kind=kCustom, calls=%fused_computation.1 | custom fusion | bytes 40960 | tf_op jit(solution)/shard_map/jit(_take)/gather | solution.py:18
  146.1 0.1 stack.2
  146.2 18.0 %all_to_all.5 = bf16[16,4,2048]{2,1,0:T(4,128)(2,1)S(1)} all-to-all(bf16[16,4,2048]{2,1,0:T(4,128)(2,1)S(1)} %stack.2), channel_id=1, replica_groups=mesh['ab'=16,'cd'=16] {'ab'}, dimensions={0} | all-to-all | bytes 524288 | tf_op jit(solution)/shard_map/all_to_all | solution.py:30
  164.2 0.1 reshape.52
  164.3 6.8 %fusion.1 = f32[64,2048]{1,0:T(8,128)} fusion(bf16[64,2048]{1,0:T(8,128)(2,1)S(1)} %reshape.52, bf16[2048,2048]{1,0:T(8,128)(2,1)} %param.5), kind=kOutput, calls=%fused_computation.12 | convolution fusion | flops 536870912 | bytes 9175040 | tf_op jit(solution)/shard_map/dot_general | solution.py:28
  171.1 0.0 reduce-scatter.2.cloned.1.call-update
  171.1 83.9 %reduce-scatter.2.cloned.1.call-done = f32[64,128]{1,0:T(8,128)} async-done(((f32[64,2048]{1,0:T(8,128)}), f32[64,128]{1,0:T(8,128)}) %reduce-scatter.2.cloned.1.call-update) | async-done | bytes 32784 | tf_op jit(solution)/shard_map/reduce_scatter | solution.py:36
  255.0 1.4 convert_element_type.22
  (4 shorter events, 0.1 us)
Async XLA Ops:
  6.5 9.4 %copy-start.1 = (s32[2048]{0:T(1024)S(1)}, s32[2048]{0:T(1024)}, u32[]{:S(2)}) copy-start(s32[2048]{0:T(1024)} %param.8) | copy-start | bytes 24580
  6.5 9.4 %copy-start = (s32[2048]{0:T(1024)S(1)}, s32[2048]{0:T(1024)}, u32[]{:S(2)}) copy-start(s32[2048]{0:T(1024)} %param.7) | copy-start | bytes 24580
  6.5 91.1 %all-gather.2.cloned.1.call-start = ((), (), s32[]{:S(2)}) async-start(), calls=%async_computation.2 | async-start | bytes 6092800 | tf_op jit(solution)/shard_map/all_gather | solution.py:16
  7.3 247.7 %reduce-scatter.2.cloned.1.call-start = ((), (), s32[]{:S(2)}) async-start(), calls=%async_computation.3 | async-start | bytes 557056 | tf_op jit(solution)/shard_map/reduce_scatter | solution.py:36
Sparse Core Ops, SparseCore 0:
  9.8 87.7 all-gather.1
  171.2 83.6 reduce-scatter.1
